TPU v7x, 32 devices: a whole 2x2x4 slice. The times are simulated.
32 devices in a mesh: shard: 2 (over x), context: 4 (over y, core), tensor: 4 (over z).
Axes of the slice: x: 2, y: 2, z: 4, core: 2. Of those that a mesh axis runs over, the one named last changes fastest.
Arguments:
- tokens: bfloat16 [2, 2048, 2048], P('shard', 'context'), may hold values from -6 to 6
- block_order: int32 [2, 8], P('shard'), may hold values from 0 to 7, each once within a row
- w_query: bfloat16 [2048, 2048], P(('shard', 'context'), 'tensor'), may hold values from -0.5 to 0.5
- w_key: bfloat16 [2048, 512], P(('shard', 'context'), 'tensor'), may hold values from -0.5 to 0.5
- w_value: bfloat16 [2048, 512], P(('shard', 'context'), 'tensor'), may hold values from -0.125 to 0.125
- w_output: bfloat16 [2048, 2048], P('tensor', ('shard', 'context')), may hold values from -1.5 to 1.5
- w_gate: bfloat16 [2048, 8192], P(('shard', 'context'), 'tensor'), may hold values from -0.125 to 0.125
- w_up: bfloat16 [2048, 8192], P(('shard', 'context'), 'tensor'), may hold values from -0.125 to 0.125
- w_down: bfloat16 [8192, 2048], P('tensor', ('shard', 'context')), may hold values from -0.5 to 0.5
- norm_attn: bfloat16 [2048], P(('shard', 'context')), may hold values from 0.5 to 1.5
- norm_ffn: bfloat16 [2048], P(('shard', 'context')), may hold values from 0.5 to 1.5
- grad_out: bfloat16 [2, 2048, 2048], P('shard', 'context'), may hold values from -6 to 6
Outputs:
- layer_out: bfloat16 [2, 2048, 2048], P('shard', 'context')
- grad_tokens: float32 [2, 2048, 2048], P('shard', 'context')
- grad_w_query: float32 [2048, 2048], P(('shard', 'context'), 'tensor')
- grad_w_key: float32 [2048, 512], P(('shard', 'context'), 'tensor')
- grad_w_value: float32 [2048, 512], P(('shard', 'context'), 'tensor')
- grad_w_output: float32 [2048, 2048], P('tensor', ('shard', 'context'))
- grad_w_gate: float32 [2048, 8192], P(('shard', 'context'), 'tensor')
- grad_w_up: float32 [2048, 8192], P(('shard', 'context'), 'tensor')
- grad_w_down: float32 [8192, 2048], P('tensor', ('shard', 'context'))
- grad_norm_attn: float32 [2048], P(('shard', 'context'))
- grad_norm_ffn: float32 [2048], P(('shard', 'context'))
Inputs may be any that keep to these rules, and one draw needn't show every extreme that they name: Each row is a permutation of the 8 blocks of its sequence; stored block j of sequence s holds the tokens of block block_order[s, j].
All inputs are finite; a program needn't handle non-finite values.
Results may differ from a plain program's by a relative error of at most 0.015.
Values may be sent and summed in bfloat16 or wider, within the bound.
A program may use at most 192 MiB of HBM per device.

v0:
```python
import math
import jax
import jax.numpy as jnp
from jax import lax
from jax.sharding import PartitionSpec as P

HD = 64
BLK = 256
EPSILON = 1e-05
SCORE_SCALE = 0.015625
RESIDUAL_SCALE = 0.22
ROPE_BASE = 10000000.0
MASKED_SCORE = -1e30


def rope_tables(placed):
    half_dim = HD // 2
    inverse = jnp.exp(jnp.arange(half_dim, dtype=jnp.float32) * (-2.0 * math.log(ROPE_BASE) / HD))
    angles = placed.astype(jnp.float32)[:, None] * inverse[None, :]
    angles = jnp.concatenate([angles, angles], axis=1)
    return (jnp.cos(angles), jnp.sin(angles))


def rotate(values, cosine, sine):
    half_dim = values.shape[-1] // 2
    turned = jnp.concatenate([-values[..., half_dim:], values[..., :half_dim]], axis=-1)
    return values * cosine[:, None, :] + turned * sine[:, None, :]


def rms_norm(values, gain):
    return values * lax.rsqrt(jnp.mean(values * values, axis=-1, keepdims=True) + EPSILON) * gain


def stored_places(order_row, first, count):
    stored = first + jnp.arange(count, dtype=jnp.int32)
    picks = (stored // BLK)[:, None] == jnp.arange(order_row.shape[0], dtype=jnp.int32)[None, :]
    return jnp.sum(jnp.where(picks, order_row[None, :], 0), axis=1) * BLK + stored % BLK


def fetch_weights(w_query, w_key, w_value, w_output, w_gate, w_up, w_down, norm_attn, norm_ffn):
    return (
        lax.all_gather(w_query, ("shard", "context"), axis=0, tiled=True),
        lax.all_gather(w_key, ("shard", "context"), axis=0, tiled=True),
        lax.all_gather(w_value, ("shard", "context"), axis=0, tiled=True),
        lax.all_gather(w_output, ("shard", "context"), axis=1, tiled=True),
        lax.all_gather(w_gate, ("shard", "context"), axis=0, tiled=True),
        lax.all_gather(w_up, ("shard", "context"), axis=0, tiled=True),
        lax.all_gather(w_down, ("shard", "context"), axis=1, tiled=True),
        lax.all_gather(norm_attn, ("shard", "context"), axis=0, tiled=True),
        lax.all_gather(norm_ffn, ("shard", "context"), axis=0, tiled=True),
    )


def branch_total(partial_sum):
    return lax.psum(partial_sum, "tensor")


def norm_total(partial_sum):
    return lax.psum(partial_sum, "tensor")


def to_rows(items, seq_count, kv_count, group_size, local_len):
    head_dim = items.shape[-1]
    shaped = items.reshape(seq_count, kv_count, group_size, local_len, head_dim).transpose(
        0, 3, 1, 2, 4
    )
    return shaped.reshape(seq_count * local_len, kv_count * group_size * head_dim)


def from_rows(rows_in, seq_count, kv_count, group_size, local_len):
    shaped = rows_in.reshape(seq_count, local_len, kv_count, group_size, HD).transpose(
        0, 2, 3, 1, 4
    )
    return shaped.reshape(seq_count * kv_count, group_size * local_len, HD)


def softmax_rows(query_rows, key_rows, query_block, key_block):
    scores = SCORE_SCALE * jnp.einsum(
        "qd,kd->qk", query_rows, key_rows, preferred_element_type=jnp.float32
    )
    scores = jnp.where(key_block[None, :] <= query_block[:, None], scores, MASKED_SCORE)
    row_max = jnp.max(scores, axis=1, keepdims=True)
    exponent = jnp.exp(scores - row_max)
    return exponent / jnp.sum(exponent, axis=1, keepdims=True)


def attend_forward(packed, exact):
    query_rows, key_rows, value_rows, query_block, key_block = packed
    soft_weights = softmax_rows(query_rows, key_rows, query_block, key_block)
    rounded = soft_weights.astype(jnp.bfloat16)
    mixture = jnp.dot(rounded, value_rows, preferred_element_type=jnp.float32)
    if exact:
        remainder = (soft_weights - rounded.astype(jnp.float32)).astype(jnp.bfloat16)
        return (
            mixture,
            mixture + jnp.dot(remainder, value_rows, preferred_element_type=jnp.float32),
        )
    return (mixture, mixture)


def attend_backward(packed):
    query_rows, key_rows, value_rows, query_block, key_block, exact_rows, grad_rows = packed
    soft_weights = softmax_rows(query_rows, key_rows, query_block, key_block)
    grad_soft = jnp.einsum("qd,kd->qk", grad_rows, value_rows, preferred_element_type=jnp.float32)
    inner = jnp.sum(grad_rows.astype(jnp.float32) * exact_rows, axis=1, keepdims=True)
    grad_scores = (soft_weights * (grad_soft - inner)).astype(jnp.bfloat16)
    grad_query = SCORE_SCALE * jnp.dot(grad_scores, key_rows, preferred_element_type=jnp.float32)
    grad_key = SCORE_SCALE * jnp.einsum(
        "qk,qd->kd", grad_scores, query_rows, preferred_element_type=jnp.float32
    )
    grad_value = jnp.einsum(
        "qk,qd->kd",
        soft_weights.astype(jnp.bfloat16),
        grad_rows,
        preferred_element_type=jnp.float32,
    )
    return (grad_query, grad_key, grad_value)


def layer_pass(tokens_f, order, weight_set, exact):
    w_query, w_key, w_value, w_output, w_gate, w_up, w_down, norm_attn, norm_ffn = weight_set
    seq_count = order.shape[0]
    row_count = tokens_f.shape[0]
    local_len = row_count // seq_count
    full_len = local_len * lax.axis_size("context")
    first = lax.axis_index("context") * local_len
    q_places = jnp.stack([stored_places(order[0], first, local_len)])
    k_places = jnp.stack([stored_places(order[0], 0, full_len)])
    cosine, sine = rope_tables(q_places.reshape(-1))
    head_count = w_query.shape[1] // HD
    kv_count = w_key.shape[1] // HD
    group_size = head_count // kv_count
    normed = rms_norm(tokens_f, norm_attn.astype(jnp.float32)).astype(jnp.bfloat16)
    query_lin = jnp.dot(normed, w_query, preferred_element_type=jnp.float32)
    key_lin = jnp.dot(normed, w_key, preferred_element_type=jnp.float32)
    value_low = jnp.dot(normed, w_value, preferred_element_type=jnp.float32).astype(jnp.bfloat16)
    query_rot = rotate(query_lin.reshape(row_count, head_count, HD), cosine, sine).astype(
        jnp.bfloat16
    )
    key_rot = rotate(key_lin.reshape(row_count, kv_count, HD), cosine, sine).astype(jnp.bfloat16)
    key_all, value_all = (
        lax.all_gather(
            key_rot.reshape(seq_count, local_len, kv_count * HD), "context", axis=1, tiled=True
        ),
        lax.all_gather(
            value_low.reshape(seq_count, local_len, kv_count * HD), "context", axis=1, tiled=True
        ),
    )
    item_count = seq_count * kv_count
    query_items = from_rows(
        query_rot.reshape(row_count, head_count * HD), seq_count, kv_count, group_size, local_len
    )
    key_items = (
        key_all.reshape(seq_count, full_len, kv_count, HD)
        .transpose(0, 2, 1, 3)
        .reshape(item_count, full_len, HD)
    )
    value_items = (
        value_all.reshape(seq_count, full_len, kv_count, HD)
        .transpose(0, 2, 1, 3)
        .reshape(item_count, full_len, HD)
    )
    query_block = jnp.repeat(jnp.tile(q_places // BLK, (1, group_size)), kv_count, axis=0)
    key_block = jnp.repeat(k_places // BLK, kv_count, axis=0)
    mixture, exact_mix = lax.map(
        lambda packed: attend_forward(packed, exact),
        (query_items, key_items, value_items, query_block, key_block),
    )
    mixed_low = to_rows(mixture, seq_count, kv_count, group_size, local_len).astype(jnp.bfloat16)
    branch = branch_total(jnp.dot(mixed_low, w_output, preferred_element_type=jnp.float32))
    hidden = tokens_f + RESIDUAL_SCALE * branch
    normed_ffn = rms_norm(hidden, norm_ffn.astype(jnp.float32)).astype(jnp.bfloat16)
    gate_in = jnp.dot(normed_ffn, w_gate, preferred_element_type=jnp.float32)
    upward = jnp.dot(normed_ffn, w_up, preferred_element_type=jnp.float32)
    active = (jax.nn.silu(gate_in) * upward).astype(jnp.bfloat16)
    saved = (
        normed,
        cosine,
        sine,
        query_items,
        key_items,
        value_items,
        query_block,
        key_block,
        exact_mix,
        mixed_low,
        hidden,
        normed_ffn,
        gate_in,
        upward,
        active,
    )
    if exact:
        return (hidden, saved)
    layer_out = hidden + RESIDUAL_SCALE * branch_total(
        jnp.dot(active, w_down, preferred_element_type=jnp.float32)
    )
    return (layer_out, saved)


def local(
    tokens,
    block_order,
    w_query,
    w_key,
    w_value,
    w_output,
    w_gate,
    w_up,
    w_down,
    norm_attn,
    norm_ffn,
    grad_out,
):
    seq_count, local_len, width = tokens.shape
    row_count = seq_count * local_len
    tokens_f = tokens.reshape(row_count, width).astype(jnp.float32)
    gathered = fetch_weights(
        w_query, w_key, w_value, w_output, w_gate, w_up, w_down, norm_attn, norm_ffn
    )
    layer_out, unused_saved = layer_pass(tokens_f, block_order, gathered, False)
    again = fetch_weights(
        w_query, w_key, w_value, w_output, w_gate, w_up, w_down, norm_attn, norm_ffn
    )
    unused_hidden, saved = layer_pass(tokens_f, block_order, again, True)
    (
        normed,
        cosine,
        sine,
        query_items,
        key_items,
        value_items,
        query_block,
        key_block,
        exact_mix,
        mixed_low,
        hidden,
        normed_ffn,
        gate_in,
        upward,
        active,
    ) = saved
    (
        full_query,
        full_key,
        full_value,
        full_output,
        full_gate,
        full_up,
        full_down,
        full_norm_attn,
        full_norm_ffn,
    ) = again
    head_count = full_query.shape[1] // HD
    kv_count = full_key.shape[1] // HD
    group_size = head_count // kv_count
    full_len = key_items.shape[1]
    grad_rows = grad_out.reshape(row_count, width).astype(jnp.float32)
    d_ffn = (RESIDUAL_SCALE * grad_rows).astype(jnp.bfloat16)
    grad_down = jnp.einsum("rf,rd->fd", active, d_ffn, preferred_element_type=jnp.float32)
    d_active = jnp.einsum("rd,fd->rf", d_ffn, full_down, preferred_element_type=jnp.float32)
    unused_product, silu_pull = jax.vjp(
        lambda left, right: jax.nn.silu(left) * right, gate_in, upward
    )
    d_gate, d_upward = silu_pull(d_active)
    d_gate = d_gate.astype(jnp.bfloat16)
    d_upward = d_upward.astype(jnp.bfloat16)
    grad_gate = jnp.einsum("rd,rf->df", normed_ffn, d_gate, preferred_element_type=jnp.float32)
    grad_up = jnp.einsum("rd,rf->df", normed_ffn, d_upward, preferred_element_type=jnp.float32)
    d_normed_ffn = norm_total(
        jnp.einsum("rf,df->rd", d_gate, full_gate, preferred_element_type=jnp.float32)
        + jnp.einsum("rf,df->rd", d_upward, full_up, preferred_element_type=jnp.float32)
    )
    unused_norm, ffn_pull = jax.vjp(rms_norm, hidden, full_norm_ffn.astype(jnp.float32))
    d_hidden, grad_norm_ffn = ffn_pull(d_normed_ffn)
    d_hidden = grad_rows + d_hidden
    d_branch = (RESIDUAL_SCALE * d_hidden).astype(jnp.bfloat16)
    grad_output = jnp.einsum("rh,rd->hd", mixed_low, d_branch, preferred_element_type=jnp.float32)
    d_mixed = jnp.einsum(
        "rd,hd->rh", d_branch, full_output, preferred_element_type=jnp.float32
    ).astype(jnp.bfloat16)
    grad_items = from_rows(d_mixed, seq_count, kv_count, group_size, local_len)
    grad_query_items, grad_key_items, grad_value_items = lax.map(
        attend_backward,
        (query_items, key_items, value_items, query_block, key_block, exact_mix, grad_items),
    )
    key_grads = (
        grad_key_items.reshape(seq_count, kv_count, full_len, HD)
        .transpose(0, 2, 1, 3)
        .reshape(seq_count, full_len, kv_count * HD)
    )
    value_grads = (
        grad_value_items.reshape(seq_count, kv_count, full_len, HD)
        .transpose(0, 2, 1, 3)
        .reshape(seq_count, full_len, kv_count * HD)
    )
    key_local, value_local = (
        lax.psum_scatter(key_grads, "context", scatter_dimension=1, tiled=True),
        lax.psum_scatter(value_grads, "context", scatter_dimension=1, tiled=True),
    )
    query_back = to_rows(grad_query_items, seq_count, kv_count, group_size, local_len).reshape(
        row_count, head_count, HD
    )
    d_query = (
        rotate(query_back, cosine, -sine).reshape(row_count, head_count * HD).astype(jnp.bfloat16)
    )
    d_key = (
        rotate(key_local.reshape(row_count, kv_count, HD), cosine, -sine)
        .reshape(row_count, kv_count * HD)
        .astype(jnp.bfloat16)
    )
    d_value = value_local.reshape(row_count, kv_count * HD).astype(jnp.bfloat16)
    grad_query = jnp.einsum("rd,rh->dh", normed, d_query, preferred_element_type=jnp.float32)
    grad_key = jnp.einsum("rd,rh->dh", normed, d_key, preferred_element_type=jnp.float32)
    grad_value = jnp.einsum("rd,rh->dh", normed, d_value, preferred_element_type=jnp.float32)
    d_normed = norm_total(
        jnp.einsum("rh,dh->rd", d_query, full_query, preferred_element_type=jnp.float32)
        + jnp.einsum("rh,dh->rd", d_key, full_key, preferred_element_type=jnp.float32)
        + jnp.einsum("rh,dh->rd", d_value, full_value, preferred_element_type=jnp.float32)
    )
    unused_first, attn_pull = jax.vjp(rms_norm, tokens_f, full_norm_attn.astype(jnp.float32))
    d_tokens, grad_norm_attn = attn_pull(d_normed)
    grad_tokens = d_hidden + d_tokens
    reduced = (
        lax.psum_scatter(grad_query, ("shard", "context"), scatter_dimension=0, tiled=True),
        lax.psum_scatter(grad_key, ("shard", "context"), scatter_dimension=0, tiled=True),
        lax.psum_scatter(grad_value, ("shard", "context"), scatter_dimension=0, tiled=True),
        lax.psum_scatter(grad_output, ("shard", "context"), scatter_dimension=1, tiled=True),
        lax.psum_scatter(grad_gate, ("shard", "context"), scatter_dimension=0, tiled=True),
        lax.psum_scatter(grad_up, ("shard", "context"), scatter_dimension=0, tiled=True),
        lax.psum_scatter(grad_down, ("shard", "context"), scatter_dimension=1, tiled=True),
        lax.psum_scatter(grad_norm_attn, ("shard", "context"), scatter_dimension=0, tiled=True),
        lax.psum_scatter(grad_norm_ffn, ("shard", "context"), scatter_dimension=0, tiled=True),
    )
    return (
        layer_out.reshape(seq_count, local_len, width).astype(jnp.bfloat16),
        grad_tokens.reshape(seq_count, local_len, width),
        reduced[0],
        reduced[1],
        reduced[2],
        reduced[3],
        reduced[4],
        reduced[5],
        reduced[6],
        reduced[7],
        reduced[8],
    )


def solution(mesh):
    return jax.shard_map(
        local,
        mesh=mesh,
        in_specs=(
            P("shard", "context", None),
            P("shard", None),
            P(("shard", "context"), "tensor"),
            P(("shard", "context"), "tensor"),
            P(("shard", "context"), "tensor"),
            P("tensor", ("shard", "context")),
            P(("shard", "context"), "tensor"),
            P(("shard", "context"), "tensor"),
            P("tensor", ("shard", "context")),
            P(("shard", "context")),
            P(("shard", "context")),
            P("shard", "context", None),
        ),
        out_specs=(
            P("shard", "context", None),
            P("shard", "context", None),
            P(("shard", "context"), "tensor"),
            P(("shard", "context"), "tensor"),
            P(("shard", "context"), "tensor"),
            P("tensor", ("shard", "context")),
            P(("shard", "context"), "tensor"),
            P(("shard", "context"), "tensor"),
            P("tensor", ("shard", "context")),
            P(("shard", "context")),
            P(("shard", "context")),
        ),
        check_vma=False,
    )
```

profile of v0, /device:TPU:0, one launch (start us, length us, event | category | flops | bytes accessed | tf_op | source)
XLA Modules:
  0.0 1781.7 jit_solution(12693808725064753597)
XLA Ops:
  13.1 10.4 all-gather.1
  25.4 11.1 all_gather.46
  36.5 9.5 all_gather.48
  61.0 10.2 all_gather.47
  84.2 51.4 %while.37 = (s32[]{:T(128)}, bf16[2,2048,64]{1,2,0:T(8,128)(2,1)}, f32[2,2048,64]{1,2,0:T(8,128)}, s32[2,2048]{1,0:T(2,128)S(1)}, s32[2,2048]{1,0:T(2,128)S(1)},...) while((s32[]{:T(128)}, bf16[2,2048,64]{1,2,0:T(8,128)(2,1)}, ...), condition=%wide.region_13.14_spmd, body=%wide.region_10.13_spmd.sunk | while | flops 1690431488 | bytes 184675568 | solution.py:165
  156.3 26.2 %while.36 = (s32[]{:T(128)}, bf16[2,2048,64]{1,2,0:T(8,128)(2,1)}, s32[2,2048]{1,0:T(2,128)S(1)}, s32[2,2048]{1,0:T(2,128)S(1)}, bf16[2,2048,64]{2,1,0:T(8,128)(...) while((s32[]{:T(128)}, bf16[2,2048,64]{1,2,0:T(8,128)(2,1)}, ...), condition=%wide.region_6.7_spmd, body=%wide.region_3.6_spmd.sunk | while | flops 1136652288 | bytes 56748184 | solution.py:165
  192.3 108.3 %all-reduce.9.cloned.1.call-done = f32[512,2048]{1,0:T(8,128)} async-done(((f32[512,2048]{1,0:T(8,128)}), f32[512,2048]{1,0:T(8,128)}) %all-reduce.9.cloned.1.call-update) | async-done | bytes 4194320 | tf_op jit(solution)/shard_map/psum | solution.py:55
  306.4 49.2 %all-gather.13.cloned.1.call-done = bf16[2048,2048]{1,0:T(8,128)(2,1)} async-done(((bf16[256,2048]{1,0:T(8,128)(2,1)}), bf16[2048,2048]{1,0:T(8,128)(2,1)}) %all-gather.13.cloned.1.call-update) | async-done | bytes 8388624 | tf_op jit(solution)/shard_map/all_gather | solution.py:46
  355.6 10.5 fusion.175
  366.1 45.5 %all-gather.15.cloned.1.call-done = bf16[2048,2048]{1,0:T(8,128)(2,1)} async-done(((bf16[256,2048]{1,0:T(8,128)(2,1)}), bf16[2048,2048]{1,0:T(8,128)(2,1)}) %all-gather.15.cloned.1.call-update) | async-done | bytes 8388624 | tf_op jit(solution)/shard_map/all_gather | solution.py:47
  411.6 10.5 fusion.174
  422.1 47.1 %all-gather.17.cloned.1.call-done = bf16[2048,2048]{1,0:T(8,128)(2,1)} async-done(((bf16[2048,256]{1,0:T(8,128)(2,1)}), bf16[2048,2048]{1,0:T(8,128)(2,1)}) %all-gather.17.cloned.1.call-update) | async-done | bytes 8388624 | tf_op jit(solution)/shard_map/all_gather | solution.py:48
  469.2 12.3 multiply_convert_fusion.3
  481.6 11.1 fusion.176
  500.8 291.0 %all-reduce.13.cloned.1.call-done = (f32[512,2048]{1,0:T(8,128)}, f32[512,2048]{1,0:T(8,128)}) async-done(((f32[512,2048]{1,0:T(8,128)}, f32[512,2048]{1,0:T(8,128)}), (f32[512,2048]{1,0:T(8,128)}, f32[512,2048]{1,0:T(8,128)})) %all-reduce.13.cloned.1.call-update) | async-done | bytes 8388624 | tf_op jit(solution)/shard_map/psum | solution.py:59
  812.1 65.3 %while.38 = (s32[]{:T(128)}, f32[2,2048,64]{1,2,0:T(8,128)}, f32[2,2048,64]{1,2,0:T(8,128)}, f32[2,2048,64]{1,2,0:T(8,128)}, s32[2,2048]{1,0:T(2,128)S(1)}, /*in...) while((s32[]{:T(128)}, f32[2,2048,64]{1,2,0:T(8,128)}, ...), condition=%wide.region_22.23_spmd, body=%wide.region_18.22_spmd.sunk | while | flops 2781472768 | bytes 199144912 | solution.py:283
  829.9 9.5 multiply_convert_fusion.11
  862.3 9.5 multiply_convert_fusion.11
  878.2 10.8 fusion.171
  889.0 18.3 %fusion.172 = f32[512,2048]{1,0:T(8,128)} fusion(bf16[2048,2048]{1,0:T(8,128)(2,1)} %all-gather.17.cloned.1.call-done, f32[512,2048]{1,0:T(8,128)} %fusion.171, bf16[512,2048]{1,0:T(8,128)(2,1)S(1)} %copy-done.38, bf16[2048,2048]{1,0:T(8,128)(2,1)} %all-gather.15.cloned.1.call-done), kind=kOutput, calls=%fused_computation.249 | convolution fusion | flops 8596226048 | bytes 27262976 | tf_op jit(solution)/shard_map/dot_general | solution.py:196
  918.8 9.8 reduce-scatter.12.cloned.1.call-done
  952.8 14.6 fusion.97
  967.7 12.6 fusion.180
  980.4 12.6 fusion.179
  994.9 231.0 %all-reduce.11.cloned.1.call-done = (f32[512,2048]{1,0:T(8,128)}, f32[512,2048]{1,0:T(8,128)}) async-done(((f32[512,2048]{1,0:T(8,128)}, f32[512,2048]{1,0:T(8,128)}), (f32[512,2048]{1,0:T(8,128)}, f32[512,2048]{1,0:T(8,128)})) %all-reduce.11.cloned.1.call-update) | async-done | bytes 8388624 | tf_op jit(solution)/shard_map/psum | solution.py:55
  1229.4 24.1 %all-reduce.2 = (f32[2048]{0:T(1024)S(1)}, f32[2048]{0:T(1024)S(1)}) all-reduce(f32[2048]{0:T(1024)S(1)} %get-tuple-element.235, f32[2048]{0:T(1024)S(1)} %copy-done.51), channel_id=12, replica_groups=mesh['shard'=2,'context'=4,'tensor'=4] {'shard','context'}, use_global_device_ids=true, to_apply=%region_35.36.clone | all-reduce | flops 4096 | bytes 32768
  1264.7 39.6 %reduce-scatter.18.cloned.1.call-done = f32[256,128]{1,0:T(8,128)} async-done(((f32[2048,128]{1,0:T(8,128)}), f32[256,128]{1,0:T(8,128)}) %reduce-scatter.18.cloned.1.call-update) | async-done | bytes 131088 | tf_op jit(solution)/shard_map/reduce_scatter | solution.py:327
  1304.3 55.0 %reduce-scatter.20.cloned.1.call-done = f32[512,256]{1,0:T(8,128)} async-done(((f32[512,2048]{1,0:T(8,128)}), f32[512,256]{1,0:T(8,128)}) %reduce-scatter.20.cloned.1.call-update) | async-done | bytes 524304 | tf_op jit(solution)/shard_map/reduce_scatter | solution.py:328
  1359.3 55.0 %reduce-scatter.14.cloned.1.call-done = f32[256,512]{1,0:T(8,128)} async-done(((f32[2048,512]{1,0:T(8,128)}), f32[256,512]{1,0:T(8,128)}) %reduce-scatter.14.cloned.1.call-update) | async-done | bytes 524304 | tf_op jit(solution)/shard_map/reduce_scatter | solution.py:325
  1414.3 120.0 %reduce-scatter.26.cloned.1.call-done = f32[2048,256]{1,0:T(8,128)} async-done(((f32[2048,2048]{1,0:T(8,128)}), f32[2048,256]{1,0:T(8,128)}) %reduce-scatter.26.cloned.1.call-update) | async-done | bytes 2097168 | tf_op jit(solution)/shard_map/reduce_scatter | solution.py:331
  1534.3 120.2 %reduce-scatter.24.cloned.1.call-done = f32[256,2048]{1,0:T(8,128)} async-done(((f32[2048,2048]{1,0:T(8,128)}), f32[256,2048]{1,0:T(8,128)}) %reduce-scatter.24.cloned.1.call-update) | async-done | bytes 2097168 | tf_op jit(solution)/shard_map/reduce_scatter | solution.py:330
  1654.5 120.2 %reduce-scatter.22.cloned.1.call-done = f32[256,2048]{1,0:T(8,128)} async-done(((f32[2048,2048]{1,0:T(8,128)}), f32[256,2048]{1,0:T(8,128)}) %reduce-scatter.22.cloned.1.call-update) | async-done | bytes 2097168 | tf_op jit(solution)/shard_map/reduce_scatter | solution.py:329
  (309 shorter events, 274.7 us)
Async XLA Ops:
  7.2 39.6 %copy-start.2 = (bf16[1,512,2048]{2,1,0:T(8,128)(2,1)S(1)}, bf16[1,512,2048]{2,1,0:T(8,128)(2,1)}, u32[]{:S(2)}) copy-start(bf16[1,512,2048]{2,1,0:T(8,128)(2,1)} %param.18) | copy-start | bytes 6291460
  7.2 29.3 %copy-start.48 = (bf16[256,128]{1,0:T(8,128)(2,1)S(1)}, bf16[256,128]{1,0:T(8,128)(2,1)}, u32[]{:S(2)}) copy-start(bf16[256,128]{1,0:T(8,128)(2,1)} %param.22) | copy-start | bytes 196612
  7.2 65.9 %all-gather.9.cloned.1.call-start = ((), (), s32[]{:S(2)}) async-start(), calls=%async_computation.9 | async-start | bytes 2359296 | tf_op jit(solution)/shard_map/all_gather | solution.py:42
  7.9 131.8 %all-gather.11.cloned.1.call-start = ((), (), s32[]{:S(2)}) async-start(), calls=%async_computation.10 | async-start | bytes 2359296 | tf_op jit(solution)/shard_map/all_gather | solution.py:45
  8.7 291.9 %all-reduce.9.cloned.1.call-start = ((), (), s32[]{:S(2)}) async-start(), calls=%async_computation.14 | async-start | bytes 8388608 | tf_op jit(solution)/shard_map/psum | solution.py:55
  12.4 65.0 %copy-start.49 = (f32[512]{0:T(512)}, f32[512]{0:T(512)S(1)}, u32[]{:S(2)}) copy-start(f32[512]{0:T(512)S(1)} %fusion.153) | copy-start | bytes 6148
  23.6 53.8 %copy-start.44 = (f32[8,1,256]{2,1,0:T(1,128)}, f32[8,1,256]{2,1,0:T(1,128)S(1)}, u32[]{:S(2)}) copy-start(f32[8,1,256]{2,1,0:T(1,128)S(1)} %convert_element_type.206) | copy-start | bytes 24580
  25.4 55.1 %copy-start.22 = (f32[512,64]{0,1:T(8,128)}, f32[512,64]{0,1:T(8,128)S(1)}, u32[]{:S(2)}) copy-start(f32[512,64]{0,1:T(8,128)S(1)} %get-tuple-element.334) | copy-start | bytes 393220
  36.5 24.4 %copy-start.25 = (bf16[2048,128]{1,0:T(8,128)(2,1)}, bf16[2048,128]{1,0:T(8,128)(2,1)S(1)}, u32[]{:S(2)}) copy-start(bf16[2048,128]{1,0:T(8,128)(2,1)S(1)} %all_gather.46) | copy-start | bytes 1572868
  144.8 210.8 %all-gather.13.cloned.1.call-start = ((), (), s32[]{:S(2)}) async-start(), calls=%async_computation.11 | async-start | bytes 9437184 | tf_op jit(solution)/shard_map/all_gather | solution.py:46
  145.4 266.2 %all-gather.15.cloned.1.call-start = ((), (), s32[]{:S(2)}) async-start(), calls=%async_computation.12 | async-start | bytes 9437184 | tf_op jit(solution)/shard_map/all_gather | solution.py:47
  146.0 323.2 %all-gather.17.cloned.1.call-start = ((), (), s32[]{:S(2)}) async-start(), calls=%async_computation.13 | async-start | bytes 9437184 | tf_op jit(solution)/shard_map/all_gather | solution.py:48
  146.6 645.2 %all-reduce.13.cloned.1.call-start = ((), (), s32[]{:S(2)}) async-start(), calls=%async_computation.25 | async-start | bytes 16777216 | tf_op jit(solution)/shard_map/psum | solution.py:59
  186.1 114.5 %copy-start.3 = (bf16[1,512,2048]{2,1,0:T(8,128)(2,1)S(1)}, bf16[1,512,2048]{2,1,0:T(8,128)(2,1)}, u32[]{:S(2)}) copy-start(bf16[1,512,2048]{2,1,0:T(8,128)(2,1)} %param.18) | copy-start | bytes 6291460
  192.3 111.4 %copy-start.47 = (f32[8,1,256]{2,1,0:T(1,128)S(1)}, f32[8,1,256]{2,1,0:T(1,128)}, u32[]{:S(2)}) copy-start(f32[8,1,256]{2,1,0:T(1,128)} %convert_element_type.207) | copy-start | bytes 24580
  481.5 11.1 copy-start.57
  481.5 11.1 copy-start.58
  481.5 11.1 copy-start.54
  500.7 413.1 %reduce-scatter.10.cloned.1.call-start = ((), (), s32[]{:S(2)}) async-start(), calls=%async_computation.15 | async-start | bytes 1310720 | tf_op jit(solution)/shard_map/reduce_scatter | solution.py:298
  877.4 51.3 %reduce-scatter.12.cloned.1.call-start = ((), (), s32[]{:S(2)}) async-start(), calls=%async_computation.16 | async-start | bytes 1310720 | tf_op jit(solution)/shard_map/reduce_scatter | solution.py:299
  878.1 347.8 %all-reduce.11.cloned.1.call-start = ((), (), s32[]{:S(2)}) async-start(), calls=%async_computation.24 | async-start | bytes 16777216 | tf_op jit(solution)/shard_map/psum | solution.py:55
  889.0 18.3 %copy-start.35 = (f32[2,2048,64]{1,2,0:T(8,128)S(1)}, f32[2,2048,64]{1,2,0:T(8,128)}, u32[]{:S(2)}) copy-start(f32[2,2048,64]{1,2,0:T(8,128)} %get-tuple-element.153) | copy-start | bytes 3145732
  913.8 14.9 copy-start.41
  934.9 329.7 %reduce-scatter.16.cloned.1.call-start = ((), (), s32[]{:S(2)}) async-start(), calls=%async_computation.18 | async-start | bytes 1179648 | tf_op jit(solution)/shard_map/reduce_scatter | solution.py:326
  938.6 365.7 %reduce-scatter.18.cloned.1.call-start = ((), (), s32[]{:S(2)}) async-start(), calls=%async_computation.19 | async-start | bytes 1179648 | tf_op jit(solution)/shard_map/reduce_scatter | solution.py:327
  940.6 418.7 %reduce-scatter.20.cloned.1.call-start = ((), (), s32[]{:S(2)}) async-start(), calls=%async_computation.20 | async-start | bytes 4718592 | tf_op jit(solution)/shard_map/reduce_scatter | solution.py:328
  946.3 468.0 %reduce-scatter.14.cloned.1.call-start = ((), (), s32[]{:S(2)}) async-start(), calls=%async_computation.17 | async-start | bytes 4718592 | tf_op jit(solution)/shard_map/reduce_scatter | solution.py:325
  952.7 581.6 %reduce-scatter.26.cloned.1.call-start = ((), (), s32[]{:S(2)}) async-start(), calls=%async_computation.23 | async-start | bytes 18874368 | tf_op jit(solution)/shard_map/reduce_scatter | solution.py:331
  967.4 687.1 %reduce-scatter.24.cloned.1.call-start = ((), (), s32[]{:S(2)}) async-start(), calls=%async_computation.22 | async-start | bytes 18874368 | tf_op jit(solution)/shard_map/reduce_scatter | solution.py:330
  980.4 794.4 %reduce-scatter.22.cloned.1.call-start = ((), (), s32[]{:S(2)}) async-start(), calls=%async_computation.21 | async-start | bytes 18874368 | tf_op jit(solution)/shard_map/reduce_scatter | solution.py:329
  993.0 236.4 %copy-start.51 = (f32[2048]{0:T(1024)S(1)}, f32[2048]{0:T(1024)}, u32[]{:S(2)}) copy-start(f32[2048]{0:T(1024)} %get-tuple-element.233) | copy-start | bytes 24580
  993.1 261.7 %copy-start.53 = (f32[512]{0:T(512)S(1)}, f32[512]{0:T(512)}, u32[]{:S(2)}) copy-start(f32[512]{0:T(512)} %copy-done.52) | copy-start | bytes 6148
  (61 other events, 247.9 us)
Sparse Core Ops, SparseCore 0:
  9.9 31.1 all-gather.8
  43.0 31.8 all-gather.10
  144.9 155.5 all-reduce.8
  302.3 53.2 all-gather.12
  357.3 54.2 all-gather.14
  413.3 55.8 all-gather.16
  500.8 290.8 all-reduce.12
  877.5 23.7 reduce-scatter.9
  903.8 24.7 reduce-scatter.11
  935.0 290.8 all-reduce.10
  1229.7 34.9 reduce-scatter.15
  1268.3 35.9 reduce-scatter.17
  1308.2 51.0 reduce-scatter.19
  1363.1 51.1 reduce-scatter.13
  1418.3 115.9 reduce-scatter.25
  1538.3 116.1 reduce-scatter.23
  1658.5 116.1 reduce-scatter.21
where the time goes:
time: 1790 us; the launch traced here: 1780 us
  waiting for transfers between devices  1300 us (73%)
  matrix products  234 us (13%)
  other arithmetic  89.3 us (5%)
  blocking collectives  82.9 us (5%)
  local copies, waits for them, and re-layouts  61.1 us (3%)
    psum x2, waiting for transfers between devices, branch_total(): return lax.psum(partial_sum, 'tensor')  339 us
    psum x1, waiting for transfers between devices, norm_total(): return lax.psum(partial_sum, 'tensor')  291 us
    reduce_scatter x1, waiting for transfers between devices, local(): lax.psum_scatter(grad_up, ('shard', 'context'), scatter_dimension=0, tile...  120 us
    reduce_scatter x1, waiting for transfers between devices, local(): lax.psum_scatter(grad_gate, ('shard', 'context'), scatter_dimension=0, ti...  120 us
    reduce_scatter x1, waiting for transfers between devices, local(): lax.psum_scatter(grad_down, ('shard', 'context'), scatter_dimension=1, ti...  120 us
    reduce_scatter x1, waiting for transfers between devices, local(): lax.psum_scatter(grad_output, ('shard', 'context'), scatter_dimension=1,...  55 us
    reduce_scatter x1, waiting for transfers between devices, local(): lax.psum_scatter(grad_query, ('shard', 'context'), scatter_dimension=0, t...  55 us
    all_gather x1, waiting for transfers between devices, fetch_weights(): lax.all_gather(w_gate, ('shard', 'context'), axis=0, tiled=True)  49.2 us
  transfers between devices with their start and end apart: 17, of which 14 were waited for; matrix products, arithmetic and copies ran while one was open for 13% of the time, Pallas kernels for 0%

commit v1 on v0

--- a/solution.py
+++ b/solution.py
@@ -52,7 +52,7 @@
 
 
 def branch_total(partial_sum):
-    return lax.psum(partial_sum, "tensor")
+    return jnp.sum(lax.all_gather(partial_sum, "tensor"), axis=0)
 
 
 def norm_total(partial_sum):

time: 1790 us -> 2190 us (1.22)
  waiting for transfers between devices: 1300 us -> 1660 us
  other arithmetic: 89.3 us -> 124 us
    all_gather x0 -> x3, waiting for transfers between devices: none -> 749 us  [branch_total(): return jnp.sum(lax.all_gather(partial_sum, 'tensor'), axis=0)]
    psum x2 -> x0, waiting for transfers between devices: 339 us -> none  [branch_total(): return lax.psum(partial_sum, 'tensor')]
    psum x1 -> x2, waiting for transfers between devices: 291 us -> 211 us  [norm_total(): return lax.psum(partial_sum, 'tensor')]
    reduce_sum x0 -> x3, other arithmetic: none -> 30.7 us  [branch_total(): return jnp.sum(lax.all_gather(partial_sum, 'tensor'), axis=0)]
  transfers between devices with their start and end apart: 17 -> 19, of which waited for: 14 -> 17; matrix products, arithmetic and copies ran while one was open for 13% -> 14% of each run, Pallas kernels for 0% -> 0%
where the time goes in v1:
time: 2190 us; the launch traced here: 2180 us
  waiting for transfers between devices  1660 us (76%)
  matrix products  233 us (11%)
  other arithmetic  124 us (6%)
  blocking collectives  83.9 us (4%)
  local copies, waits for them, and re-layouts  60.9 us (3%)
    all_gather x3, waiting for transfers between devices, branch_total(): return jnp.sum(lax.all_gather(partial_sum, 'tensor'), axis=0)  749 us
    psum x2, waiting for transfers between devices, norm_total(): return lax.psum(partial_sum, 'tensor')  211 us
    reduce_scatter x1, waiting for transfers between devices, local(): lax.psum_scatter(grad_gate, ('shard', 'context'), scatter_dimension=0, ti...  120 us
    reduce_scatter x1, waiting for transfers between devices, local(): lax.psum_scatter(grad_up, ('shard', 'context'), scatter_dimension=0, tile...  120 us
    reduce_scatter x1, waiting for transfers between devices, local(): lax.psum_scatter(grad_down, ('shard', 'context'), scatter_dimension=1, ti...  120 us
    reduce_scatter x1, waiting for transfers between devices, local(): lax.psum_scatter(grad_query, ('shard', 'context'), scatter_dimension=0, t...  55 us
    reduce_scatter x1, waiting for transfers between devices, local(): lax.psum_scatter(grad_output, ('shard', 'context'), scatter_dimension=1,...  54.9 us
    all_gather x1, waiting for transfers between devices, fetch_weights(): lax.all_gather(w_down, ('shard', 'context'), axis=1, tiled=True)  47.1 us
  transfers between devices with their start and end apart: 19, of which 17 were waited for; matrix products, arithmetic and copies ran while one was open for 14% of the time, Pallas kernels for 0%

profile of v1, /device:TPU:0, one launch (start us, length us, event | category | flops | bytes accessed | tf_op | source)
XLA Modules:
  0.0 2184.2 jit_solution(2433461671763799129)
XLA Ops:
  13.1 10.4 all-gather.4
  25.4 11.1 all_gather.64
  84.1 51.4 %while.37 = (s32[]{:T(128)}, bf16[2,2048,64]{1,2,0:T(8,128)(2,1)}, f32[2,2048,64]{1,2,0:T(8,128)}, s32[2,2048]{1,0:T(2,128)S(1)}, s32[2,2048]{1,0:T(2,128)S(1)},...) while((s32[]{:T(128)}, bf16[2,2048,64]{1,2,0:T(8,128)(2,1)}, ...), condition=%wide.region_13.14_spmd, body=%wide.region_10.13_spmd.sunk | while | flops 1690431488 | bytes 184675568 | solution.py:165
  146.5 25.9 %while.36 = (s32[]{:T(128)}, bf16[2,2048,64]{1,2,0:T(8,128)(2,1)}, s32[2,2048]{1,0:T(2,128)S(1)}, s32[2,2048]{1,0:T(2,128)S(1)}, bf16[2,2048,64]{2,1,0:T(8,128)(...) while((s32[]{:T(128)}, bf16[2,2048,64]{1,2,0:T(8,128)(2,1)}, ...), condition=%wide.region_6.7_spmd, body=%wide.region_3.6_spmd.sunk | while | flops 1136652288 | bytes 56748184 | solution.py:165
  190.7 241.5 %all-gather.29.cloned.1.call-done = f32[2048,2048]{1,0:T(8,128)} async-done(((f32[512,2048]{1,0:T(8,128)}), f32[2048,2048]{1,0:T(8,128)}) %all-gather.29.cloned.1.call-update) | async-done | bytes 16777232 | tf_op jit(solution)/shard_map/all_gather | solution.py:55
  432.3 10.3 reduce_sum.153
  448.4 38.0 %all-gather.19.cloned.1.call-done = bf16[2048,2048]{1,0:T(8,128)(2,1)} async-done(((bf16[256,2048]{1,0:T(8,128)(2,1)}), bf16[2048,2048]{1,0:T(8,128)(2,1)}) %all-gather.19.cloned.1.call-update) | async-done | bytes 8388624 | tf_op jit(solution)/shard_map/all_gather | solution.py:46
  486.5 10.5 fusion.176
  497.0 45.5 %all-gather.21.cloned.1.call-done = bf16[2048,2048]{1,0:T(8,128)(2,1)} async-done(((bf16[256,2048]{1,0:T(8,128)(2,1)}), bf16[2048,2048]{1,0:T(8,128)(2,1)}) %all-gather.21.cloned.1.call-update) | async-done | bytes 8388624 | tf_op jit(solution)/shard_map/all_gather | solution.py:47
  542.5 10.5 fusion.175
  553.0 47.1 %all-gather.23.cloned.1.call-done = bf16[2048,2048]{1,0:T(8,128)(2,1)} async-done(((bf16[2048,256]{1,0:T(8,128)(2,1)}), bf16[2048,2048]{1,0:T(8,128)(2,1)}) %all-gather.23.cloned.1.call-update) | async-done | bytes 8388624 | tf_op jit(solution)/shard_map/all_gather | solution.py:48
  600.1 12.2 multiply_convert_fusion.3
  612.4 11.8 fusion.177
  632.3 256.1 %all-gather.25.cloned.1.call-done = f32[2048,2048]{1,0:T(8,128)} async-done(((f32[512,2048]{1,0:T(8,128)}), f32[2048,2048]{1,0:T(8,128)}) %all-gather.25.cloned.1.call-update) | async-done | bytes 16777232 | tf_op jit(solution)/shard_map/all_gather | solution.py:55
  898.7 145.3 %all-reduce.6.cloned.1.call-done = f32[512,2048]{1,0:T(8,128)} async-done(((f32[512,2048]{1,0:T(8,128)}), f32[512,2048]{1,0:T(8,128)}) %all-reduce.6.cloned.1.call-update) | async-done | bytes 4194320 | tf_op jit(solution)/shard_map/psum | solution.py:59
  1064.4 65.3 %while.38 = (s32[]{:T(128)}, f32[2,2048,64]{1,2,0:T(8,128)}, f32[2,2048,64]{1,2,0:T(8,128)}, f32[2,2048,64]{1,2,0:T(8,128)}, s32[2,2048]{1,0:T(2,128)S(1)}, /*in...) while((s32[]{:T(128)}, f32[2,2048,64]{1,2,0:T(8,128)}, ...), condition=%wide.region_22.23_spmd, body=%wide.region_18.22_spmd.sunk | while | flops 2781472768 | bytes 199144912 | solution.py:283
  1137.9 15.6 reduce-scatter.10.cloned.1.call-done
  1158.5 22.2 %reduce-scatter.12.cloned.1.call-done = f32[1,512,128]{1,2,0:T(8,128)} async-done(((f32[1,2048,128]{1,2,0:T(8,128)}), f32[1,512,128]{1,2,0:T(8,128)}) %reduce-scatter.12.cloned.1.call-update) | async-done | bytes 262160 | tf_op jit(solution)/shard_map/reduce_scatter | solution.py:299
  1198.1 18.1 fusion.173
  1233.9 14.6 fusion.98
  1248.6 12.5 fusion.181
  1261.4 13.4 fusion.180
  1276.7 65.6 %all-reduce.8.cloned.1.call-done = f32[512,2048]{1,0:T(8,128)} async-done(((f32[512,2048]{1,0:T(8,128)}), f32[512,2048]{1,0:T(8,128)}) %all-reduce.8.cloned.1.call-update) | async-done | bytes 4194320 | tf_op jit(solution)/shard_map/psum | solution.py:59
  1345.8 24.6 %all-reduce.2 = (f32[2048]{0:T(1024)S(1)}, f32[2048]{0:T(1024)S(1)}) all-reduce(f32[2048]{0:T(1024)S(1)} %get-tuple-element.235, f32[2048]{0:T(1024)S(1)} %copy-done.48), channel_id=15, replica_groups=mesh['shard'=2,'context'=4,'tensor'=4] {'shard','context'}, use_global_device_ids=true, to_apply=%region_35.36.clone | all-reduce | flops 4096 | bytes 32768
  1378.3 251.2 %all-gather.27.cloned.1.call-done = f32[2048,2048]{1,0:T(8,128)} async-done(((f32[512,2048]{1,0:T(8,128)}), f32[2048,2048]{1,0:T(8,128)}) %all-gather.27.cloned.1.call-update) | async-done | bytes 16777232 | tf_op jit(solution)/shard_map/all_gather | solution.py:55
  1645.8 21.6 reduce-scatter.16.cloned.1.call-done
  1667.4 39.6 %reduce-scatter.18.cloned.1.call-done = f32[256,128]{1,0:T(8,128)} async-done(((f32[2048,128]{1,0:T(8,128)}), f32[256,128]{1,0:T(8,128)}) %reduce-scatter.18.cloned.1.call-update) | async-done | bytes 131088 | tf_op jit(solution)/shard_map/reduce_scatter | solution.py:327
  1707.0 54.9 %reduce-scatter.20.cloned.1.call-done = f32[512,256]{1,0:T(8,128)} async-done(((f32[512,2048]{1,0:T(8,128)}), f32[512,256]{1,0:T(8,128)}) %reduce-scatter.20.cloned.1.call-update) | async-done | bytes 524304 | tf_op jit(solution)/shard_map/reduce_scatter | solution.py:328
  1761.9 55.0 %reduce-scatter.14.cloned.1.call-done = f32[256,512]{1,0:T(8,128)} async-done(((f32[2048,512]{1,0:T(8,128)}), f32[256,512]{1,0:T(8,128)}) %reduce-scatter.14.cloned.1.call-update) | async-done | bytes 524304 | tf_op jit(solution)/shard_map/reduce_scatter | solution.py:325
  1816.8 120.0 %reduce-scatter.26.cloned.1.call-done = f32[2048,256]{1,0:T(8,128)} async-done(((f32[2048,2048]{1,0:T(8,128)}), f32[2048,256]{1,0:T(8,128)}) %reduce-scatter.26.cloned.1.call-update) | async-done | bytes 2097168 | tf_op jit(solution)/shard_map/reduce_scatter | solution.py:331
  1936.9 120.2 %reduce-scatter.24.cloned.1.call-done = f32[256,2048]{1,0:T(8,128)} async-done(((f32[2048,2048]{1,0:T(8,128)}), f32[256,2048]{1,0:T(8,128)}) %reduce-scatter.24.cloned.1.call-update) | async-done | bytes 2097168 | tf_op jit(solution)/shard_map/reduce_scatter | solution.py:330
  2057.1 120.4 %reduce-scatter.22.cloned.1.call-done = f32[256,2048]{1,0:T(8,128)} async-done(((f32[2048,2048]{1,0:T(8,128)}), f32[256,2048]{1,0:T(8,128)}) %reduce-scatter.22.cloned.1.call-update) | async-done | bytes 2097168 | tf_op jit(solution)/shard_map/reduce_scatter | solution.py:329
  (313 shorter events, 347.3 us)
Async XLA Ops:
  7.2 39.6 %copy-start.2 = (bf16[1,512,2048]{2,1,0:T(8,128)(2,1)S(1)}, bf16[1,512,2048]{2,1,0:T(8,128)(2,1)}, u32[]{:S(2)}) copy-start(bf16[1,512,2048]{2,1,0:T(8,128)(2,1)} %param.18) | copy-start | bytes 6291460
  7.2 29.3 %copy-start.45 = (bf16[256,128]{1,0:T(8,128)(2,1)S(1)}, bf16[256,128]{1,0:T(8,128)(2,1)}, u32[]{:S(2)}) copy-start(bf16[256,128]{1,0:T(8,128)(2,1)} %param.22) | copy-start | bytes 196612
  7.2 65.9 %all-gather.15.cloned.1.call-start = ((), (), s32[]{:S(2)}) async-start(), calls=%async_computation.9 | async-start | bytes 2359296 | tf_op jit(solution)/shard_map/all_gather | solution.py:42
  7.9 131.7 %all-gather.17.cloned.1.call-start = ((), (), s32[]{:S(2)}) async-start(), calls=%async_computation.10 | async-start | bytes 2359296 | tf_op jit(solution)/shard_map/all_gather | solution.py:45
  8.7 423.6 %all-gather.29.cloned.1.call-start = ((), (), s32[]{:S(2)}) async-start(), calls=%async_computation.27 | async-start | bytes 20971520 | tf_op jit(solution)/shard_map/all_gather | solution.py:55
  12.4 64.9 %copy-start.46 = (f32[512]{0:T(512)}, f32[512]{0:T(512)S(1)}, u32[]{:S(2)}) copy-start(f32[512]{0:T(512)S(1)} %fusion.154) | copy-start | bytes 6148
  23.6 53.7 %copy-start.42 = (f32[8,1,256]{2,1,0:T(1,128)}, f32[8,1,256]{2,1,0:T(1,128)S(1)}, u32[]{:S(2)}) copy-start(f32[8,1,256]{2,1,0:T(1,128)S(1)} %convert_element_type.205) | copy-start | bytes 24580
  25.4 55.0 %copy-start.20 = (f32[512,64]{0,1:T(8,128)}, f32[512,64]{0,1:T(8,128)S(1)}, u32[]{:S(2)}) copy-start(f32[512,64]{0,1:T(8,128)S(1)} %get-tuple-element.328) | copy-start | bytes 393220
  36.5 24.4 %copy-start.22 = (bf16[2048,128]{1,0:T(8,128)(2,1)}, bf16[2048,128]{1,0:T(8,128)(2,1)S(1)}, u32[]{:S(2)}) copy-start(bf16[2048,128]{1,0:T(8,128)(2,1)S(1)} %all_gather.64) | copy-start | bytes 1572868
  144.8 341.7 %all-gather.19.cloned.1.call-start = ((), (), s32[]{:S(2)}) async-start(), calls=%async_computation.11 | async-start | bytes 9437184 | tf_op jit(solution)/shard_map/all_gather | solution.py:46
  145.3 397.2 %all-gather.21.cloned.1.call-start = ((), (), s32[]{:S(2)}) async-start(), calls=%async_computation.12 | async-start | bytes 9437184 | tf_op jit(solution)/shard_map/all_gather | solution.py:47
  145.9 454.2 %all-gather.23.cloned.1.call-start = ((), (), s32[]{:S(2)}) async-start(), calls=%async_computation.13 | async-start | bytes 9437184 | tf_op jit(solution)/shard_map/all_gather | solution.py:48
  146.5 742.0 %all-gather.25.cloned.1.call-start = ((), (), s32[]{:S(2)}) async-start(), calls=%async_computation.25 | async-start | bytes 20971520 | tf_op jit(solution)/shard_map/all_gather | solution.py:55
  181.1 862.9 %all-reduce.6.cloned.1.call-start = ((), (), s32[]{:S(2)}) async-start(), calls=%async_computation.14 | async-start | bytes 8388608 | tf_op jit(solution)/shard_map/psum | solution.py:59
  612.4 11.8 copy-start.54
  612.4 11.8 copy-start.55
  632.3 521.3 %reduce-scatter.10.cloned.1.call-start = ((), (), s32[]{:S(2)}) async-start(), calls=%async_computation.15 | async-start | bytes 1310720 | tf_op jit(solution)/shard_map/reduce_scatter | solution.py:298
  1129.7 51.1 %reduce-scatter.12.cloned.1.call-start = ((), (), s32[]{:S(2)}) async-start(), calls=%async_computation.16 | async-start | bytes 1310720 | tf_op jit(solution)/shard_map/reduce_scatter | solution.py:299
  1130.3 212.0 %all-reduce.8.cloned.1.call-start = ((), (), s32[]{:S(2)}) async-start(), calls=%async_computation.17 | async-start | bytes 8388608 | tf_op jit(solution)/shard_map/psum | solution.py:59
  1134.6 21.1 copy-start.23
  1137.9 42.8 %copy-start.39 = (bf16[2048,128]{1,0:T(8,128)(2,1)S(1)}, bf16[2048,128]{1,0:T(8,128)(2,1)}, u32[]{:S(2)}) copy-start(bf16[2048,128]{1,0:T(8,128)(2,1)} %copy-done.38) | copy-start | bytes 1572868
  1154.6 32.5 %copy-start.33 = (f32[512,2,64]{0,2,1:T(8,128)}, f32[512,2,64]{0,2,1:T(8,128)S(1)}, u32[]{:S(2)}) copy-start(f32[512,2,64]{0,2,1:T(8,128)S(1)} %maximum_multiply_fusion.2) | copy-start | bytes 786436
  1187.1 442.3 %all-gather.27.cloned.1.call-start = ((), (), s32[]{:S(2)}) async-start(), calls=%async_computation.26 | async-start | bytes 20971520 | tf_op jit(solution)/shard_map/all_gather | solution.py:55
  1216.3 451.1 %reduce-scatter.16.cloned.1.call-start = ((), (), s32[]{:S(2)}) async-start(), calls=%async_computation.19 | async-start | bytes 1179648 | tf_op jit(solution)/shard_map/reduce_scatter | solution.py:326
  1220.2 486.8 %reduce-scatter.18.cloned.1.call-start = ((), (), s32[]{:S(2)}) async-start(), calls=%async_computation.20 | async-start | bytes 1179648 | tf_op jit(solution)/shard_map/reduce_scatter | solution.py:327
  1222.2 539.6 %reduce-scatter.20.cloned.1.call-start = ((), (), s32[]{:S(2)}) async-start(), calls=%async_computation.21 | async-start | bytes 4718592 | tf_op jit(solution)/shard_map/reduce_scatter | solution.py:328
  1227.9 588.9 %reduce-scatter.14.cloned.1.call-start = ((), (), s32[]{:S(2)}) async-start(), calls=%async_computation.18 | async-start | bytes 4718592 | tf_op jit(solution)/shard_map/reduce_scatter | solution.py:325
  1233.9 703.0 %reduce-scatter.26.cloned.1.call-start = ((), (), s32[]{:S(2)}) async-start(), calls=%async_computation.24 | async-start | bytes 18874368 | tf_op jit(solution)/shard_map/reduce_scatter | solution.py:331
  1248.5 808.5 %reduce-scatter.24.cloned.1.call-start = ((), (), s32[]{:S(2)}) async-start(), calls=%async_computation.23 | async-start | bytes 18874368 | tf_op jit(solution)/shard_map/reduce_scatter | solution.py:330
  1261.1 916.3 %reduce-scatter.22.cloned.1.call-start = ((), (), s32[]{:S(2)}) async-start(), calls=%async_computation.22 | async-start | bytes 18874368 | tf_op jit(solution)/shard_map/reduce_scatter | solution.py:329
  1274.8 71.0 %copy-start.48 = (f32[2048]{0:T(1024)S(1)}, f32[2048]{0:T(1024)}, u32[]{:S(2)}) copy-start(f32[2048]{0:T(1024)} %get-tuple-element.233) | copy-start | bytes 24580
  1274.8 96.9 %copy-start.50 = (f32[512]{0:T(512)S(1)}, f32[512]{0:T(512)}, u32[]{:S(2)}) copy-start(f32[512]{0:T(512)} %copy-done.49) | copy-start | bytes 6148
  (60 other events, 269.7 us)
Sparse Core Ops, SparseCore 0:
  9.9 31.1 all-gather.14
  43.0 31.8 all-gather.16
  144.9 287.3 all-gather.28
  434.0 52.4 all-gather.18
  488.2 54.2 all-gather.20
  544.2 55.8 all-gather.22
  601.7 286.7 all-gather.24
  890.8 153.1 all-reduce.5
  1129.8 23.7 reduce-scatter.9
  1155.9 24.7 reduce-scatter.11
  1187.3 154.9 all-reduce.7
  1343.7 285.7 all-gather.26
  1633.2 34.1 reduce-scatter.15
  1671.0 35.9 reduce-scatter.17
  1710.8 51.0 reduce-scatter.19
  1765.6 51.1 reduce-scatter.13
  1820.8 115.9 reduce-scatter.25
  1940.9 116.1 reduce-scatter.23
  2061.2 116.1 reduce-scatter.21
